TPU v7x, 128 devices: a whole 4x4x4 slice. The times are simulated.
128 devices in a mesh: row: 16 (over x, z_hi, core), col: 8 (over z_lo, y).
Axes of the slice: x: 4, y: 4, z: 4 (z_hi: 2, z_lo: 2; z = z_hi * 2 + z_lo), core: 2. Of those that a mesh axis runs over, the one named last changes fastest.
Arguments:
- pair: bfloat16 [1024, 1024, 128], P('row', 'col'), may hold values from -6 to 6
- bias_weight: bfloat16 [128, 16], replicated
- single: bfloat16 [48, 1024, 768], P('col', 'row'), may hold values from -6 to 6
- w_qkv: bfloat16 [768, 2304], replicated, may hold values from -0.21875 to 0.21875
- w_out: bfloat16 [768, 768], replicated, may hold values from -0.21875 to 0.21875
- w_gate_up: bfloat16 [768, 3072], replicated, may hold values from -0.21875 to 0.21875
- w_down: bfloat16 [1536, 768], replicated, may hold values from -0.15625 to 0.15625
- cotangent: bfloat16 [48, 1024, 768], P('col', 'row'), may hold values from -300 to 300
Outputs:
- updated: bfloat16 [48, 1024, 768], P('col', 'row')
- pair_grad: float32 [1024, 1024, 128], P('row', 'col')
All inputs are finite; a program needn't handle non-finite values.
Results may differ from a plain program's by a relative error of at most 0.012.
The roundings to bfloat16 on the way count: a program that leaves them out, or rounds other values in their place, can miss the bound.
Values may be sent and summed in bfloat16 or wider, within the bound.
No kernel may reach another device: no remote copies, remote signals or barrier semaphores. Data moves between devices by JAX's collectives and lax.ppermute only.
A program may use at most 192 MiB of HBM per device.

v0:
```python
import math
import jax
import jax.numpy as jnp
from jax import lax
from jax.sharding import PartitionSpec as P


def normalize(values):
    mean_val = jnp.mean(values, axis=-1, keepdims=True)
    centred = values - mean_val
    variance = jnp.mean(centred * centred, axis=-1, keepdims=True)
    scaled = lax.rsqrt(variance + 1e-05)
    return (centred * scaled, scaled)


def project_pair(piece, bias_weight):
    normed_pair, scaled = normalize(piece.astype(jnp.float32))
    row_count, col_count, chans = normed_pair.shape
    flat = jnp.dot(
        normed_pair.reshape(row_count * col_count, chans),
        bias_weight.astype(jnp.float32),
        precision=lax.Precision.HIGHEST,
    )
    return jnp.transpose(flat.reshape(row_count, col_count, -1), (2, 0, 1)).astype(jnp.bfloat16)


def attend_sample(queries, key_rows, value_rows, cotan, bias, head_count):
    row_count, width = queries.shape
    head_size = width // head_count
    query_h = queries.reshape(row_count, head_count, head_size)
    key_h = key_rows.reshape(-1, head_count, head_size)
    value_h = value_rows.reshape(-1, head_count, head_size)
    cotan_h = cotan.reshape(row_count, head_count, head_size)
    scores = jnp.einsum(
        "ihe,jhe->hij", query_h, key_h, preferred_element_type=jnp.float32
    ) / math.sqrt(head_size) + bias.astype(jnp.float32)
    weights = jax.nn.softmax(scores, axis=-1)
    rounded = weights.astype(jnp.bfloat16)
    attended = jnp.einsum("hij,jhe->ihe", rounded, value_h, preferred_element_type=jnp.float32)
    dprob = jnp.einsum("ihe,jhe->hij", cotan_h, value_h, preferred_element_type=jnp.float32)
    row_delta = jnp.sum(cotan_h.astype(jnp.float32) * attended, axis=2)
    grad_term = weights * (dprob - jnp.transpose(row_delta)[:, :, None])
    return (attended.reshape(row_count, width), grad_term)


def transition(single, attended, w_out, w_gate_up, w_down):
    width = single.shape[-1]
    flat_in = single.reshape(-1, width).astype(jnp.float32)
    mid = flat_in + jnp.dot(
        attended.reshape(-1, width).astype(jnp.bfloat16), w_out, preferred_element_type=jnp.float32
    )
    normed_mid = normalize(mid)[0].astype(jnp.bfloat16)
    gate_up = jnp.dot(normed_mid, w_gate_up, preferred_element_type=jnp.float32)
    half = gate_up.shape[1] // 2
    hidden = (jax.nn.silu(gate_up[:, :half]) * gate_up[:, half:]).astype(jnp.bfloat16)
    result = mid + jnp.dot(hidden, w_down, preferred_element_type=jnp.float32)
    return result.astype(jnp.bfloat16).reshape(single.shape)


def back_norm(normed_grad, normed_pair, scaled):
    centred = normed_grad - jnp.mean(normed_grad, axis=-1, keepdims=True)
    along = jnp.mean(normed_grad * normed_pair, axis=-1, keepdims=True)
    return (centred - normed_pair * along) * scaled


def shards(pair, bias_weight, single, w_qkv, w_out, w_gate_up, w_down, cotangent):
    width = single.shape[2]
    head_count = bias_weight.shape[1]
    samp_count, row_count = (single.shape[0], single.shape[1])
    bias = lax.all_gather(project_pair(pair, bias_weight), "col", axis=2, tiled=True)
    normed = normalize(single.astype(jnp.float32))[0].astype(jnp.bfloat16)
    flat_normed = normed.reshape(samp_count * row_count, width)
    queries = jnp.dot(flat_normed, w_qkv[:, :width], preferred_element_type=jnp.float32).astype(
        jnp.bfloat16
    )
    queries = queries.reshape(samp_count, row_count, width)
    w_kv = w_qkv[:, width:]
    kv_local = jnp.dot(flat_normed, w_kv, preferred_element_type=jnp.float32).astype(jnp.bfloat16)
    kv_local = kv_local.reshape(samp_count, row_count, 2 * width)
    kv_all = lax.all_gather(kv_local, "row", axis=1, tiled=True)

    def one_sample(carry, inputs):
        query_s, kv_s, cotan_s = inputs
        attended, grad_term = attend_sample(
            query_s, kv_s[:, :width], kv_s[:, width:], cotan_s, bias, head_count
        )
        return (carry + grad_term, attended)

    start_grad = jnp.zeros((head_count, row_count, kv_all.shape[1]), jnp.float32)
    grad_local, attended = lax.scan(one_sample, start_grad, (queries, kv_all, cotangent))
    updated = transition(single, attended, w_out, w_gate_up, w_down)
    bias_grad = lax.psum_scatter(grad_local, "col", scatter_dimension=2, tiled=True)
    normed_pair, scaled = normalize(pair.astype(jnp.float32))
    col_count, chans = (pair.shape[1], pair.shape[2])
    flat_grad = jnp.transpose(bias_grad, (1, 2, 0)).reshape(row_count * col_count, head_count)
    normed_grad = jnp.dot(
        flat_grad, jnp.transpose(bias_weight.astype(jnp.float32)), precision=lax.Precision.HIGHEST
    )
    normed_grad = normed_grad.reshape(row_count, col_count, chans)
    pair_grad = back_norm(normed_grad, normed_pair, scaled)
    return (updated, pair_grad)


def solution(mesh):
    return jax.shard_map(
        shards,
        mesh=mesh,
        in_specs=(
            P("row", "col", None),
            P(),
            P("col", "row", None),
            P(),
            P(),
            P(),
            P(),
            P("col", "row", None),
        ),
        out_specs=(P("col", "row", None), P("row", "col", None)),
        check_vma=False,
    )
```

profile of v0, /device:TPU:1, one launch (start us, length us, event | category | flops | bytes accessed | tf_op | source)
XLA Modules:
  0.0 442.7 jit_solution(11677037070908961696)
XLA Ops:
  24.9 36.6 %all-gather.5.cloned.1.call-done = bf16[16,64,1024]{2,0,1:T(8,128)(2,1)} async-done(((bf16[16,64,128]{2,0,1:T(8,128)(2,1)}), bf16[16,64,1024]{2,0,1:T(8,128)(2,1)}) %all-gather.5.cloned.1.call-update) | async-done | bytes 2097168 | tf_op jit(solution)/shard_map/all_gather | solution.py:70
  65.5 124.4 %all-gather.3.cloned.1.call-done = bf16[6,1024,1536]{2,1,0:T(8,128)(2,1)} async-done(((bf16[6,64,1536]{2,1,0:T(8,128)(2,1)}), bf16[6,1024,1536]{2,1,0:T(8,128)(2,1)}) %all-gather.3.cloned.1.call-update) | async-done | bytes 18874384 | tf_op jit(solution)/shard_map/all_gather | solution.py:80
  190.0 182.2 %while.13 = (s32[]{:T(128)}, f32[16,64,1024]{2,1,0:T(8,128)}, bf16[6,64,768]{2,1,0:T(8,128)(2,1)}, bf16[6,64,768]{2,1,0:T(8,128)(2,1)}, bf16[6,1024,1536]{2,1,0:...) while((s32[]{:T(128)}, f32[16,64,1024]{2,1,0:T(8,128)}, ...), condition=%wide.region_8.9_spmd.clone, body=%wide.region_4.8_spmd.clone.sunk | while | flops 314769408 | bytes 48255596 | solution.py:90
  194.9 4.7 %copy.59 = bf16[1,1024,1536]{1,2,0:T(8,128)(2,1)} copy(bf16[1,1024,1536]{2,1,0:T(8,128)(2,1)} %constant_dynamic-slice_fusion.6) | data formatting | bytes 6291456 | tf_op jit(solution)/shard_map/while/body/jit(dynamic_index_in_dim)/dynamic_slice | solution.py:90
  203.4 5.7 %fusion.69 = (f32[16,64]{1,0:T(8,128)S(1)}, f32[16,64,1024]{2,1,0:T(8,128)}) fusion(bf16[16,64,1024]{2,1,0:T(8,128)(2,1)} %get-tuple-element.206, bf16[64,16,48]{0,2,1:T(8,128)(2,1)S(1)} %bitcast.70, bf16[1024,16,48]{0,2,1:T(8,128)(2,1)} %bitcast.67), kind=kOutput, calls=%fused_computation.64.clone.1 | convolution fusion | flops 105907200 | bytes 7966720 | tf_op jit(solution)/shard_map/while/body/eval_jaxpr/sub | solution.py:37
  212.8 5.8 %select_add_fusion.2 = f32[16,64,1024]{2,1,0:T(8,128)} fusion(f32[16,64,1024]{2,1,0:T(8,128)} %get-tuple-element.193, bf16[64,16,48]{0,2,1:T(8,128)(2,1)S(1)} %bitcast.73, bf16[1024,16,48]{0,2,1:T(8,128)(2,1)} %bitcast.69, f32[16,64]{1,0:T(8,128)S(1)} %bitcast.82, pred[]{:T(512)S(6)} %compare.3, f32[16,64,1024]{2,1,0:T(8,128)} %get-tuple-element.179, ...), kind=kOutput, calls=%fused_computation.1.clone.1 | convolution fusion | flops 105906176 | bytes 14262273 | tf_op jit(solution)/shard_map/while/body/eval_jaxpr/ihe,jhe->hij/dot_general | solution.py:40
  224.2 4.7 %copy.59 = bf16[1,1024,1536]{1,2,0:T(8,128)(2,1)} copy(bf16[1,1024,1536]{2,1,0:T(8,128)(2,1)} %constant_dynamic-slice_fusion.6) | data formatting | bytes 6291456 | tf_op jit(solution)/shard_map/while/body/jit(dynamic_index_in_dim)/dynamic_slice | solution.py:90
  232.8 5.7 %fusion.69 = (f32[16,64]{1,0:T(8,128)S(1)}, f32[16,64,1024]{2,1,0:T(8,128)}) fusion(bf16[16,64,1024]{2,1,0:T(8,128)(2,1)} %get-tuple-element.206, bf16[64,16,48]{0,2,1:T(8,128)(2,1)S(1)} %bitcast.70, bf16[1024,16,48]{0,2,1:T(8,128)(2,1)} %bitcast.67), kind=kOutput, calls=%fused_computation.64.clone.1 | convolution fusion | flops 105907200 | bytes 7966720 | tf_op jit(solution)/shard_map/while/body/eval_jaxpr/sub | solution.py:37
  242.1 7.0 %select_add_fusion.2 = f32[16,64,1024]{2,1,0:T(8,128)} fusion(f32[16,64,1024]{2,1,0:T(8,128)} %get-tuple-element.193, bf16[64,16,48]{0,2,1:T(8,128)(2,1)S(1)} %bitcast.73, bf16[1024,16,48]{0,2,1:T(8,128)(2,1)} %bitcast.69, f32[16,64]{1,0:T(8,128)S(1)} %bitcast.82, pred[]{:T(512)S(6)} %compare.3, f32[16,64,1024]{2,1,0:T(8,128)} %get-tuple-element.179, ...), kind=kOutput, calls=%fused_computation.1.clone.1 | convolution fusion | flops 105906176 | bytes 14262273 | tf_op jit(solution)/shard_map/while/body/eval_jaxpr/ihe,jhe->hij/dot_general | solution.py:40
  254.8 4.7 %copy.59 = bf16[1,1024,1536]{1,2,0:T(8,128)(2,1)} copy(bf16[1,1024,1536]{2,1,0:T(8,128)(2,1)} %constant_dynamic-slice_fusion.6) | data formatting | bytes 6291456 | tf_op jit(solution)/shard_map/while/body/jit(dynamic_index_in_dim)/dynamic_slice | solution.py:90
  263.4 5.7 %fusion.69 = (f32[16,64]{1,0:T(8,128)S(1)}, f32[16,64,1024]{2,1,0:T(8,128)}) fusion(bf16[16,64,1024]{2,1,0:T(8,128)(2,1)} %get-tuple-element.206, bf16[64,16,48]{0,2,1:T(8,128)(2,1)S(1)} %bitcast.70, bf16[1024,16,48]{0,2,1:T(8,128)(2,1)} %bitcast.67), kind=kOutput, calls=%fused_computation.64.clone.1 | convolution fusion | flops 105907200 | bytes 7966720 | tf_op jit(solution)/shard_map/while/body/eval_jaxpr/sub | solution.py:37
  272.7 7.0 %select_add_fusion.2 = f32[16,64,1024]{2,1,0:T(8,128)} fusion(f32[16,64,1024]{2,1,0:T(8,128)} %get-tuple-element.193, bf16[64,16,48]{0,2,1:T(8,128)(2,1)S(1)} %bitcast.73, bf16[1024,16,48]{0,2,1:T(8,128)(2,1)} %bitcast.69, f32[16,64]{1,0:T(8,128)S(1)} %bitcast.82, pred[]{:T(512)S(6)} %compare.3, f32[16,64,1024]{2,1,0:T(8,128)} %get-tuple-element.179, ...), kind=kOutput, calls=%fused_computation.1.clone.1 | convolution fusion | flops 105906176 | bytes 14262273 | tf_op jit(solution)/shard_map/while/body/eval_jaxpr/ihe,jhe->hij/dot_general | solution.py:40
  285.3 4.7 %copy.59 = bf16[1,1024,1536]{1,2,0:T(8,128)(2,1)} copy(bf16[1,1024,1536]{2,1,0:T(8,128)(2,1)} %constant_dynamic-slice_fusion.6) | data formatting | bytes 6291456 | tf_op jit(solution)/shard_map/while/body/jit(dynamic_index_in_dim)/dynamic_slice | solution.py:90
  293.9 5.7 %fusion.69 = (f32[16,64]{1,0:T(8,128)S(1)}, f32[16,64,1024]{2,1,0:T(8,128)}) fusion(bf16[16,64,1024]{2,1,0:T(8,128)(2,1)} %get-tuple-element.206, bf16[64,16,48]{0,2,1:T(8,128)(2,1)S(1)} %bitcast.70, bf16[1024,16,48]{0,2,1:T(8,128)(2,1)} %bitcast.67), kind=kOutput, calls=%fused_computation.64.clone.1 | convolution fusion | flops 105907200 | bytes 7966720 | tf_op jit(solution)/shard_map/while/body/eval_jaxpr/sub | solution.py:37
  303.3 7.0 %select_add_fusion.2 = f32[16,64,1024]{2,1,0:T(8,128)} fusion(f32[16,64,1024]{2,1,0:T(8,128)} %get-tuple-element.193, bf16[64,16,48]{0,2,1:T(8,128)(2,1)S(1)} %bitcast.73, bf16[1024,16,48]{0,2,1:T(8,128)(2,1)} %bitcast.69, f32[16,64]{1,0:T(8,128)S(1)} %bitcast.82, pred[]{:T(512)S(6)} %compare.3, f32[16,64,1024]{2,1,0:T(8,128)} %get-tuple-element.179, ...), kind=kOutput, calls=%fused_computation.1.clone.1 | convolution fusion | flops 105906176 | bytes 14262273 | tf_op jit(solution)/shard_map/while/body/eval_jaxpr/ihe,jhe->hij/dot_general | solution.py:40
  315.9 4.7 %copy.59 = bf16[1,1024,1536]{1,2,0:T(8,128)(2,1)} copy(bf16[1,1024,1536]{2,1,0:T(8,128)(2,1)} %constant_dynamic-slice_fusion.6) | data formatting | bytes 6291456 | tf_op jit(solution)/shard_map/while/body/jit(dynamic_index_in_dim)/dynamic_slice | solution.py:90
  324.5 5.7 %fusion.69 = (f32[16,64]{1,0:T(8,128)S(1)}, f32[16,64,1024]{2,1,0:T(8,128)}) fusion(bf16[16,64,1024]{2,1,0:T(8,128)(2,1)} %get-tuple-element.206, bf16[64,16,48]{0,2,1:T(8,128)(2,1)S(1)} %bitcast.70, bf16[1024,16,48]{0,2,1:T(8,128)(2,1)} %bitcast.67), kind=kOutput, calls=%fused_computation.64.clone.1 | convolution fusion | flops 105907200 | bytes 7966720 | tf_op jit(solution)/shard_map/while/body/eval_jaxpr/sub | solution.py:37
  333.8 7.0 %select_add_fusion.2 = f32[16,64,1024]{2,1,0:T(8,128)} fusion(f32[16,64,1024]{2,1,0:T(8,128)} %get-tuple-element.193, bf16[64,16,48]{0,2,1:T(8,128)(2,1)S(1)} %bitcast.73, bf16[1024,16,48]{0,2,1:T(8,128)(2,1)} %bitcast.69, f32[16,64]{1,0:T(8,128)S(1)} %bitcast.82, pred[]{:T(512)S(6)} %compare.3, f32[16,64,1024]{2,1,0:T(8,128)} %get-tuple-element.179, ...), kind=kOutput, calls=%fused_computation.1.clone.1 | convolution fusion | flops 105906176 | bytes 14262273 | tf_op jit(solution)/shard_map/while/body/eval_jaxpr/ihe,jhe->hij/dot_general | solution.py:40
  346.5 4.7 %copy.59 = bf16[1,1024,1536]{1,2,0:T(8,128)(2,1)} copy(bf16[1,1024,1536]{2,1,0:T(8,128)(2,1)} %constant_dynamic-slice_fusion.6) | data formatting | bytes 6291456 | tf_op jit(solution)/shard_map/while/body/jit(dynamic_index_in_dim)/dynamic_slice | solution.py:90
  355.1 5.7 %fusion.69 = (f32[16,64]{1,0:T(8,128)S(1)}, f32[16,64,1024]{2,1,0:T(8,128)}) fusion(bf16[16,64,1024]{2,1,0:T(8,128)(2,1)} %get-tuple-element.206, bf16[64,16,48]{0,2,1:T(8,128)(2,1)S(1)} %bitcast.70, bf16[1024,16,48]{0,2,1:T(8,128)(2,1)} %bitcast.67), kind=kOutput, calls=%fused_computation.64.clone.1 | convolution fusion | flops 105907200 | bytes 7966720 | tf_op jit(solution)/shard_map/while/body/eval_jaxpr/sub | solution.py:37
  364.4 7.0 %select_add_fusion.2 = f32[16,64,1024]{2,1,0:T(8,128)} fusion(f32[16,64,1024]{2,1,0:T(8,128)} %get-tuple-element.193, bf16[64,16,48]{0,2,1:T(8,128)(2,1)S(1)} %bitcast.73, bf16[1024,16,48]{0,2,1:T(8,128)(2,1)} %bitcast.69, f32[16,64]{1,0:T(8,128)S(1)} %bitcast.82, pred[]{:T(512)S(6)} %compare.3, f32[16,64,1024]{2,1,0:T(8,128)} %get-tuple-element.179, ...), kind=kOutput, calls=%fused_computation.1.clone.1 | convolution fusion | flops 105906176 | bytes 14262273 | tf_op jit(solution)/shard_map/while/body/eval_jaxpr/ihe,jhe->hij/dot_general | solution.py:40
  381.3 41.4 %reduce-scatter.2.cloned.1.call-done = f32[16,64,128]{2,1,0:T(8,128)} async-done(((f32[16,64,1024]{2,1,0:T(8,128)}), f32[16,64,128]{2,1,0:T(8,128)}) %reduce-scatter.2.cloned.1.call-update) | async-done | bytes 524304 | tf_op jit(solution)/shard_map/reduce_scatter | solution.py:92
  422.7 4.6 %fusion.40 = (f32[64,128]{1,0:T(8,128)S(1)}, f32[64,128]{1,0:T(8,128)S(1)}, f32[64,128,128]{1,2,0:T(8,128)S(1)}) fusion(f32[64,128]{1,0:T(8,128)S(1)} %add_rsqrt_fusion, f32[64,128]{1,0:T(8,128)S(1)} %broadcast_multiply_fusion.2, bf16[64,128,128]{1,2,0:T(8,128)(2,1)} %copy.27, bf16[128,16]{0,1:T(8,128)(2,1)S(1)} %copy-done.5, f32[64,128,16]{1,0,2:T(8,128)} %bitcast.79), kind=kOutput, calls=%fused_computation.62 | convolution fusion | flops 207601664 | bytes 6950912 | tf_op jit(solution)/shard_map/dot_general | solution.py:96
  430.5 5.6 %copy.35 = f32[64,128,128]{2,1,0:T(8,128)} copy(f32[64,128,128]{1,2,0:T(8,128)} %fusion.17) | data formatting | bytes 8388608
  (90 shorter events, 113.1 us)
Async XLA Ops:
  7.2 371.9 %copy-start = (bf16[1536,768]{1,0:T(8,128)(2,1)S(1)}, bf16[1536,768]{1,0:T(8,128)(2,1)}, u32[]{:S(2)}) copy-start(bf16[1536,768]{1,0:T(8,128)(2,1)} %param.16) | copy-start | bytes 7077892
  7.2 54.3 %all-gather.5.cloned.1.call-start = ((), (), s32[]{:S(2)}) async-start(), calls=%async_computation.2 | async-start | bytes 2359296 | tf_op jit(solution)/shard_map/all_gather | solution.py:70
  11.4 2.3 copy-start.1
  11.4 3.1 copy-start.5
  13.7 3.5 copy-start.3
  17.2 172.8 %all-gather.3.cloned.1.call-start = ((), (), s32[]{:S(2)}) async-start(), calls=%async_computation.1 | async-start | bytes 20054016 | tf_op jit(solution)/shard_map/all_gather | solution.py:80
  17.9 4.0 copy-start.4
  21.9 400.8 %reduce-scatter.2.cloned.1.call-start = ((), (), s32[]{:S(2)}) async-start(), calls=%async_computation.3 | async-start | bytes 4718592 | tf_op jit(solution)/shard_map/reduce_scatter | solution.py:92
  422.7 4.6 %copy-start.2 = (bf16[64,128,128]{1,2,0:T(8,128)(2,1)S(1)}, bf16[64,128,128]{1,2,0:T(8,128)(2,1)}, u32[]{:S(2)}) copy-start(bf16[64,128,128]{1,2,0:T(8,128)(2,1)} %copy.27) | copy-start | bytes 6291460
Sparse Core Ops, SparseCore 0:
  17.3 44.1 all-gather.4
  64.0 125.9 all-gather.2
  372.3 50.3 reduce-scatter.1
where the time goes:
time: 444 us; the launch traced here: 443 us
  waiting for transfers between devices  202 us (45%)
  matrix products  118 us (27%)
  local copies, waits for them, and re-layouts  100 us (23%)
  between operations  13.9 us (3%)
  other arithmetic  7.22 us (2%)
    all_gather x1, waiting for transfers between devices, shards(): kv_all = lax.all_gather(kv_local, 'row', axis=1, tiled=True)  124 us
    dynamic_slice x30, local copies, waits for them, and re-layouts, shards(): lax.scan(one_sample, start_grad, (queries, kv_all, cotangent))  58.3 us
    reduce_scatter x1, waiting for transfers between devices, shards(): lax.psum_scatter(grad_local, 'col', scatter_dimension=2, tiled=True)  41.4 us
    dot_general x6, matrix products, attend_sample(): jnp.einsum('ihe,jhe->hij', cotan_h, value_h, preferred_element_type=jnp.f...  40.7 us
    all_gather x1, waiting for transfers between devices, shards(): lax.all_gather(project_pair(pair, bias_weight), 'col', axis=2, tiled=True)  36.6 us
    sub x6, matrix products, attend_sample(): weights = jax.nn.softmax(scores, axis=-1)  34.1 us
    slice x6, local copies, waits for them, and re-layouts, one_sample(): kv_s[:, :width]  23.5 us
    dot_general x6, matrix products, attend_sample(): jnp.einsum('hij,jhe->ihe', rounded, value_h, preferred_element_type=jnp.f...  20.8 us
  transfers between devices with their start and end apart: 3, of which 3 were waited for; matrix products, arithmetic and copies ran while one was open for 5% of the time, Pallas kernels for 0%

commit v1 on v0

--- a/solution.py
+++ b/solution.py
@@ -67,7 +67,12 @@
     width = single.shape[2]
     head_count = bias_weight.shape[1]
     samp_count, row_count = (single.shape[0], single.shape[1])
-    bias = lax.all_gather(project_pair(pair, bias_weight), "col", axis=2, tiled=True)
+    bias = jnp.concatenate(
+        lax.all_to_all(
+            jnp.stack([project_pair(pair, bias_weight)] * lax.axis_size("col")), "col", 0, 0
+        ),
+        axis=2,
+    )
     normed = normalize(single.astype(jnp.float32))[0].astype(jnp.bfloat16)
     flat_normed = normed.reshape(samp_count * row_count, width)
     queries = jnp.dot(flat_normed, w_qkv[:, :width], preferred_element_type=jnp.float32).astype(

time: 444 us -> 412 us (0.928)
  waiting for transfers between devices: 202 us -> 163 us
  starting transfers between devices: 0.12 us -> 6.45 us
    all_gather x1 -> x0, waiting for transfers between devices: 36.6 us -> none  [shards(): lax.all_gather(project_pair(pair, bias_weight), 'col', axis=2, tiled=True)]
    all_gather x1, waiting for transfers between devices: 124 us -> 95 us  [shards(): kv_all = lax.all_gather(kv_local, 'row', axis=1, tiled=True)]
    all_to_all x0 -> x1, waiting for transfers between devices: none -> 27.8 us  [shards(): lax.all_to_all(jnp.stack([project_pair(pair, bias_weight)] * lax.axis_siz...]
    all_to_all x0 -> x1, starting transfers between devices: none -> 6.37 us  [shards(): lax.all_to_all(jnp.stack([project_pair(pair, bias_weight)] * lax.axis_siz...]
    unnamed x15 -> x20, local copies, waits for them, and re-layouts: 13.9 us -> 10.7 us
  transfers between devices with their start and end apart: 3 -> 3, of which waited for: 3 -> 3; matrix products, arithmetic and copies ran while one was open for 5% -> 6% of each run, Pallas kernels for 0% -> 0%
where the time goes in v1:
time: 412 us; the launch traced here: 411 us
  waiting for transfers between devices  163 us (40%)
  matrix products  117 us (28%)
  local copies, waits for them, and re-layouts  98.5 us (24%)
  between operations  14.3 us (3%)
  other arithmetic  10.6 us (3%)
  starting transfers between devices  6.45 us (2%)
    all_gather x1, waiting for transfers between devices, shards(): kv_all = lax.all_gather(kv_local, 'row', axis=1, tiled=True)  95 us
    dynamic_slice x30, local copies, waits for them, and re-layouts, shards(): lax.scan(one_sample, start_grad, (queries, kv_all, cotangent))  58.3 us
    dot_general x6, matrix products, attend_sample(): jnp.einsum('ihe,jhe->hij', cotan_h, value_h, preferred_element_type=jnp.f...  40.7 us
    reduce_scatter x1, waiting for transfers between devices, shards(): lax.psum_scatter(grad_local, 'col', scatter_dimension=2, tiled=True)  40.5 us
    sub x6, matrix products, attend_sample(): weights = jax.nn.softmax(scores, axis=-1)  34.1 us
    all_to_all x1, waiting for transfers between devices, shards(): lax.all_to_all(jnp.stack([project_pair(pair, bias_weight)] * lax.axis_siz...  27.8 us
    slice x6, local copies, waits for them, and re-layouts, one_sample(): kv_s[:, :width]  23.5 us
    dot_general x6, matrix products, attend_sample(): jnp.einsum('hij,jhe->ihe', rounded, value_h, preferred_element_type=jnp.f...  20.8 us
  transfers between devices with their start and end apart: 3, of which 3 were waited for; matrix products, arithmetic and copies ran while one was open for 6% of the time, Pallas kernels for 0%

profile of v1, /device:TPU:1, one launch (start us, length us, event | category | flops | bytes accessed | tf_op | source)
XLA Modules:
  0.0 410.6 jit_solution(1937063838603152529)
XLA Ops:
  26.1 6.4 %all-to-all-start = ((bf16[8,16,64,128]{3,2,1,0:T(8,128)(2,1)}), bf16[8,16,64,128]{3,2,1,0:T(8,128)(2,1)}, u32[]{:S(2)}, u32[]{:S(2)}) async-start(bf16[8,16,64,128]{3,2,1,0:T(8,128)(2,1)} %stack.2), calls=%async_computation | async-start | bytes 4194304 | tf_op jit(solution)/shard_map/all_to_all | solution.py:71
  35.2 27.8 %all-to-all-done = bf16[8,16,64,128]{3,2,1,0:T(8,128)(2,1)} async-done(((bf16[8,16,64,128]{3,2,1,0:T(8,128)(2,1)}), bf16[8,16,64,128]{3,2,1,0:T(8,128)(2,1)}, u32[]{:S(2)}, u32[]{:S(2)}) %all-to-all-start) | async-done | bytes 2097184 | tf_op jit(solution)/shard_map/all_to_all | solution.py:71
  66.3 95.0 %all-gather.2.cloned.1.call-done = bf16[6,1024,1536]{2,1,0:T(8,128)(2,1)} async-done(((bf16[6,64,1536]{2,1,0:T(8,128)(2,1)}), bf16[6,1024,1536]{2,1,0:T(8,128)(2,1)}) %all-gather.2.cloned.1.call-update) | async-done | bytes 18874384 | tf_op jit(solution)/shard_map/all_gather | solution.py:85
  161.3 178.5 %while.13 = (s32[]{:T(128)}, f32[16,64,1024]{2,1,0:T(8,128)}, bf16[6,64,768]{2,1,0:T(8,128)(2,1)S(1)}, bf16[6,64,768]{2,1,0:T(8,128)(2,1)}, bf16[6,1024,1536]{2,...) while((s32[]{:T(128)}, f32[16,64,1024]{2,1,0:T(8,128)}, ...), condition=%wide.region_8.9_spmd.clone, body=%wide.region_4.8_spmd.clone.sunk | while | flops 314769408 | bytes 48255088 | solution.py:95
  166.2 4.7 %copy.71 = bf16[1,1024,1536]{1,2,0:T(8,128)(2,1)} copy(bf16[1,1024,1536]{2,1,0:T(8,128)(2,1)} %constant_dynamic-slice_fusion.6) | data formatting | bytes 6291456 | tf_op jit(solution)/shard_map/while/body/jit(dynamic_index_in_dim)/dynamic_slice | solution.py:95
  174.8 5.7 %fusion.70 = (f32[16,64]{1,0:T(8,128)S(1)}, f32[16,64,1024]{2,1,0:T(8,128)}) fusion(bf16[16,64,1024]{2,1,0:T(8,128)(2,1)} %get-tuple-element.215, bf16[64,16,48]{0,2,1:T(8,128)(2,1)S(1)} %bitcast.76, bf16[1024,16,48]{0,2,1:T(8,128)(2,1)} %bitcast.73), kind=kOutput, calls=%fused_computation.65.clone.1 | convolution fusion | flops 105907200 | bytes 7966720 | tf_op jit(solution)/shard_map/while/body/eval_jaxpr/sub | solution.py:37
  184.1 5.8 %select_add_fusion.2 = f32[16,64,1024]{2,1,0:T(8,128)} fusion(f32[16,64,1024]{2,1,0:T(8,128)} %get-tuple-element.202, bf16[64,16,48]{0,2,1:T(8,128)(2,1)S(1)} %bitcast.79, bf16[1024,16,48]{0,2,1:T(8,128)(2,1)} %bitcast.75, f32[16,64]{1,0:T(8,128)S(1)} %bitcast.88, pred[]{:T(512)S(6)} %compare.3, f32[16,64,1024]{2,1,0:T(8,128)} %get-tuple-element.188, ...), kind=kOutput, calls=%fused_computation.1.clone.1 | convolution fusion | flops 105906176 | bytes 14262273 | tf_op jit(solution)/shard_map/while/body/eval_jaxpr/ihe,jhe->hij/dot_general | solution.py:40
  194.9 4.7 %copy.71 = bf16[1,1024,1536]{1,2,0:T(8,128)(2,1)} copy(bf16[1,1024,1536]{2,1,0:T(8,128)(2,1)} %constant_dynamic-slice_fusion.6) | data formatting | bytes 6291456 | tf_op jit(solution)/shard_map/while/body/jit(dynamic_index_in_dim)/dynamic_slice | solution.py:95
  203.5 5.7 %fusion.70 = (f32[16,64]{1,0:T(8,128)S(1)}, f32[16,64,1024]{2,1,0:T(8,128)}) fusion(bf16[16,64,1024]{2,1,0:T(8,128)(2,1)} %get-tuple-element.215, bf16[64,16,48]{0,2,1:T(8,128)(2,1)S(1)} %bitcast.76, bf16[1024,16,48]{0,2,1:T(8,128)(2,1)} %bitcast.73), kind=kOutput, calls=%fused_computation.65.clone.1 | convolution fusion | flops 105907200 | bytes 7966720 | tf_op jit(solution)/shard_map/while/body/eval_jaxpr/sub | solution.py:37
  212.8 7.0 %select_add_fusion.2 = f32[16,64,1024]{2,1,0:T(8,128)} fusion(f32[16,64,1024]{2,1,0:T(8,128)} %get-tuple-element.202, bf16[64,16,48]{0,2,1:T(8,128)(2,1)S(1)} %bitcast.79, bf16[1024,16,48]{0,2,1:T(8,128)(2,1)} %bitcast.75, f32[16,64]{1,0:T(8,128)S(1)} %bitcast.88, pred[]{:T(512)S(6)} %compare.3, f32[16,64,1024]{2,1,0:T(8,128)} %get-tuple-element.188, ...), kind=kOutput, calls=%fused_computation.1.clone.1 | convolution fusion | flops 105906176 | bytes 14262273 | tf_op jit(solution)/shard_map/while/body/eval_jaxpr/ihe,jhe->hij/dot_general | solution.py:40
  224.9 4.7 %copy.71 = bf16[1,1024,1536]{1,2,0:T(8,128)(2,1)} copy(bf16[1,1024,1536]{2,1,0:T(8,128)(2,1)} %constant_dynamic-slice_fusion.6) | data formatting | bytes 6291456 | tf_op jit(solution)/shard_map/while/body/jit(dynamic_index_in_dim)/dynamic_slice | solution.py:95
  233.5 5.7 %fusion.70 = (f32[16,64]{1,0:T(8,128)S(1)}, f32[16,64,1024]{2,1,0:T(8,128)}) fusion(bf16[16,64,1024]{2,1,0:T(8,128)(2,1)} %get-tuple-element.215, bf16[64,16,48]{0,2,1:T(8,128)(2,1)S(1)} %bitcast.76, bf16[1024,16,48]{0,2,1:T(8,128)(2,1)} %bitcast.73), kind=kOutput, calls=%fused_computation.65.clone.1 | convolution fusion | flops 105907200 | bytes 7966720 | tf_op jit(solution)/shard_map/while/body/eval_jaxpr/sub | solution.py:37
  242.8 7.0 %select_add_fusion.2 = f32[16,64,1024]{2,1,0:T(8,128)} fusion(f32[16,64,1024]{2,1,0:T(8,128)} %get-tuple-element.202, bf16[64,16,48]{0,2,1:T(8,128)(2,1)S(1)} %bitcast.79, bf16[1024,16,48]{0,2,1:T(8,128)(2,1)} %bitcast.75, f32[16,64]{1,0:T(8,128)S(1)} %bitcast.88, pred[]{:T(512)S(6)} %compare.3, f32[16,64,1024]{2,1,0:T(8,128)} %get-tuple-element.188, ...), kind=kOutput, calls=%fused_computation.1.clone.1 | convolution fusion | flops 105906176 | bytes 14262273 | tf_op jit(solution)/shard_map/while/body/eval_jaxpr/ihe,jhe->hij/dot_general | solution.py:40
  254.8 4.7 %copy.71 = bf16[1,1024,1536]{1,2,0:T(8,128)(2,1)} copy(bf16[1,1024,1536]{2,1,0:T(8,128)(2,1)} %constant_dynamic-slice_fusion.6) | data formatting | bytes 6291456 | tf_op jit(solution)/shard_map/while/body/jit(dynamic_index_in_dim)/dynamic_slice | solution.py:95
  263.4 5.7 %fusion.70 = (f32[16,64]{1,0:T(8,128)S(1)}, f32[16,64,1024]{2,1,0:T(8,128)}) fusion(bf16[16,64,1024]{2,1,0:T(8,128)(2,1)} %get-tuple-element.215, bf16[64,16,48]{0,2,1:T(8,128)(2,1)S(1)} %bitcast.76, bf16[1024,16,48]{0,2,1:T(8,128)(2,1)} %bitcast.73), kind=kOutput, calls=%fused_computation.65.clone.1 | convolution fusion | flops 105907200 | bytes 7966720 | tf_op jit(solution)/shard_map/while/body/eval_jaxpr/sub | solution.py:37
  272.8 7.0 %select_add_fusion.2 = f32[16,64,1024]{2,1,0:T(8,128)} fusion(f32[16,64,1024]{2,1,0:T(8,128)} %get-tuple-element.202, bf16[64,16,48]{0,2,1:T(8,128)(2,1)S(1)} %bitcast.79, bf16[1024,16,48]{0,2,1:T(8,128)(2,1)} %bitcast.75, f32[16,64]{1,0:T(8,128)S(1)} %bitcast.88, pred[]{:T(512)S(6)} %compare.3, f32[16,64,1024]{2,1,0:T(8,128)} %get-tuple-element.188, ...), kind=kOutput, calls=%fused_computation.1.clone.1 | convolution fusion | flops 105906176 | bytes 14262273 | tf_op jit(solution)/shard_map/while/body/eval_jaxpr/ihe,jhe->hij/dot_general | solution.py:40
  284.8 4.7 %copy.71 = bf16[1,1024,1536]{1,2,0:T(8,128)(2,1)} copy(bf16[1,1024,1536]{2,1,0:T(8,128)(2,1)} %constant_dynamic-slice_fusion.6) | data formatting | bytes 6291456 | tf_op jit(solution)/shard_map/while/body/jit(dynamic_index_in_dim)/dynamic_slice | solution.py:95
  293.4 5.7 %fusion.70 = (f32[16,64]{1,0:T(8,128)S(1)}, f32[16,64,1024]{2,1,0:T(8,128)}) fusion(bf16[16,64,1024]{2,1,0:T(8,128)(2,1)} %get-tuple-element.215, bf16[64,16,48]{0,2,1:T(8,128)(2,1)S(1)} %bitcast.76, bf16[1024,16,48]{0,2,1:T(8,128)(2,1)} %bitcast.73), kind=kOutput, calls=%fused_computation.65.clone.1 | convolution fusion | flops 105907200 | bytes 7966720 | tf_op jit(solution)/shard_map/while/body/eval_jaxpr/sub | solution.py:37
  302.7 7.0 %select_add_fusion.2 = f32[16,64,1024]{2,1,0:T(8,128)} fusion(f32[16,64,1024]{2,1,0:T(8,128)} %get-tuple-element.202, bf16[64,16,48]{0,2,1:T(8,128)(2,1)S(1)} %bitcast.79, bf16[1024,16,48]{0,2,1:T(8,128)(2,1)} %bitcast.75, f32[16,64]{1,0:T(8,128)S(1)} %bitcast.88, pred[]{:T(512)S(6)} %compare.3, f32[16,64,1024]{2,1,0:T(8,128)} %get-tuple-element.188, ...), kind=kOutput, calls=%fused_computation.1.clone.1 | convolution fusion | flops 105906176 | bytes 14262273 | tf_op jit(solution)/shard_map/while/body/eval_jaxpr/ihe,jhe->hij/dot_general | solution.py:40
  314.8 4.7 %copy.71 = bf16[1,1024,1536]{1,2,0:T(8,128)(2,1)} copy(bf16[1,1024,1536]{2,1,0:T(8,128)(2,1)} %constant_dynamic-slice_fusion.6) | data formatting | bytes 6291456 | tf_op jit(solution)/shard_map/while/body/jit(dynamic_index_in_dim)/dynamic_slice | solution.py:95
  323.4 5.7 %fusion.70 = (f32[16,64]{1,0:T(8,128)S(1)}, f32[16,64,1024]{2,1,0:T(8,128)}) fusion(bf16[16,64,1024]{2,1,0:T(8,128)(2,1)} %get-tuple-element.215, bf16[64,16,48]{0,2,1:T(8,128)(2,1)S(1)} %bitcast.76, bf16[1024,16,48]{0,2,1:T(8,128)(2,1)} %bitcast.73), kind=kOutput, calls=%fused_computation.65.clone.1 | convolution fusion | flops 105907200 | bytes 7966720 | tf_op jit(solution)/shard_map/while/body/eval_jaxpr/sub | solution.py:37
  332.7 7.0 %select_add_fusion.2 = f32[16,64,1024]{2,1,0:T(8,128)} fusion(f32[16,64,1024]{2,1,0:T(8,128)} %get-tuple-element.202, bf16[64,16,48]{0,2,1:T(8,128)(2,1)S(1)} %bitcast.79, bf16[1024,16,48]{0,2,1:T(8,128)(2,1)} %bitcast.75, f32[16,64]{1,0:T(8,128)S(1)} %bitcast.88, pred[]{:T(512)S(6)} %compare.3, f32[16,64,1024]{2,1,0:T(8,128)} %get-tuple-element.188, ...), kind=kOutput, calls=%fused_computation.1.clone.1 | convolution fusion | flops 105906176 | bytes 14262273 | tf_op jit(solution)/shard_map/while/body/eval_jaxpr/ihe,jhe->hij/dot_general | solution.py:40
  349.8 40.5 %reduce-scatter.2.cloned.1.call-done = f32[16,64,128]{2,1,0:T(8,128)} async-done(((f32[16,64,1024]{2,1,0:T(8,128)}), f32[16,64,128]{2,1,0:T(8,128)}) %reduce-scatter.2.cloned.1.call-update) | async-done | bytes 524304 | tf_op jit(solution)/shard_map/reduce_scatter | solution.py:97
  398.2 5.6 %copy.45 = f32[64,128,128]{2,1,0:T(8,128)} copy(f32[64,128,128]{1,2,0:T(8,128)} %fusion.17) | data formatting | bytes 8388608
  (97 shorter events, 117.9 us)
Async XLA Ops:
  7.2 340.4 %copy-start = (bf16[1536,768]{1,0:T(8,128)(2,1)S(1)}, bf16[1536,768]{1,0:T(8,128)(2,1)}, u32[]{:S(2)}) copy-start(bf16[1536,768]{1,0:T(8,128)(2,1)} %param.16) | copy-start | bytes 7077892
  7.2 154.1 %all-gather.2.cloned.1.call-start = ((), (), s32[]{:S(2)}) async-start(), calls=%async_computation.2 | async-start | bytes 20054016 | tf_op jit(solution)/shard_map/all_gather | solution.py:85
  19.1 2.3 copy-start.1
  19.1 3.1 copy-start.8
  21.4 2.7 copy-start.4
  22.3 1.8 copy-start.6
  26.1 37.0 %all-to-all-start = ((bf16[8,16,64,128]{3,2,1,0:T(8,128)(2,1)}), bf16[8,16,64,128]{3,2,1,0:T(8,128)(2,1)}, u32[]{:S(2)}, u32[]{:S(2)}) async-start(bf16[8,16,64,128]{3,2,1,0:T(8,128)(2,1)} %stack.2), calls=%async_computation | async-start | bytes 4194304 | tf_op jit(solution)/shard_map/all_to_all | solution.py:71
  32.5 357.9 %reduce-scatter.2.cloned.1.call-start = ((), (), s32[]{:S(2)}) async-start(), calls=%async_computation.3 | async-start | bytes 4718592 | tf_op jit(solution)/shard_map/reduce_scatter | solution.py:97
  339.8 1.1 copy-start.3
  347.6 42.8 %copy-start.5 = (f32[64,128]{1,0:T(8,128)S(1)}, f32[64,128]{1,0:T(8,128)}, u32[]{:S(2)}) copy-start(f32[64,128]{1,0:T(8,128)} %copy-done.4) | copy-start | bytes 98308
  347.6 42.8 %copy-start.7 = (f32[64,128]{1,0:T(8,128)S(1)}, f32[64,128]{1,0:T(8,128)}, u32[]{:S(2)}) copy-start(f32[64,128]{1,0:T(8,128)} %copy-done.6) | copy-start | bytes 98308
  390.4 4.7 %copy-start.2 = (bf16[64,128,128]{1,2,0:T(8,128)(2,1)S(1)}, bf16[64,128,128]{1,2,0:T(8,128)(2,1)}, u32[]{:S(2)}) copy-start(bf16[64,128,128]{1,2,0:T(8,128)(2,1)} %copy.36) | copy-start | bytes 6291460
Sparse Core Ops, SparseCore 0:
  15.2 146.0 all-gather.1
  340.0 50.3 reduce-scatter.1
